TPU v7x, 32 devices: a whole 2x2x4 slice. The times are simulated.
32 devices in a mesh: groups: 2 (over y), seq: 4 (over z), head: 2 (over x), sub: 2 (over core).
Axes of the slice: x: 2, y: 2, z: 4, core: 2. Of those that a mesh axis runs over, the one named last changes fastest.
Arguments:
- tokens: int32 [3, 4096], P(None, ('groups', 'seq')), parts along dimension 1, may hold values from 0 to 1023
- masked: int32 [4096], P(('groups', 'seq')), parts along dimension 0, may hold values 0 or 1
- used_frames: int32 [2], P('groups'), parts along dimension 0, may hold values from 1024 to 2048
- tables: bfloat16 [3, 1024, 1024], P(None, None, ('head', 'sub')), may hold values from -6 to 6
- mask_vec: bfloat16 [1024], P(('head', 'sub')), may hold values from -6 to 6
- attn_in: bfloat16 [3, 1024, 512], P(None, None, ('head', 'sub')), may hold values from -0.1875 to 0.1875
- head_temp: float32 [8], P(('head', 'sub')), may hold values from 12 to 28
- attn_out: bfloat16 [512, 1024], P(('head', 'sub')), may hold values from -0.25 to 0.25
- conv_in: bfloat16 [2, 1024, 1024], P(None, None, ('head', 'sub')), may hold values from -0.1875 to 0.1875
- conv_kernel: float32 [31, 1024], P(None, ('head', 'sub')), may hold values from -1 to 1
- conv_out: bfloat16 [1024, 1024], P(('head', 'sub')), may hold values from -0.1875 to 0.1875
- voc_in: bfloat16 [1024, 512], P(('head', 'sub')), may hold values from -0.1875 to 0.1875
- voc_kernel: float32 [7, 512], replicated, may hold values from -2 to 2
- voc_up: bfloat16 [512, 1536], P(('head', 'sub')), may hold values from -0.25 to 0.25
- voc_down: bfloat16 [1536, 512], P(('head', 'sub')), may hold values from -0.15625 to 0.15625
- voc_head: bfloat16 [512, 1282], P(('head', 'sub')), may hold values from -0.25 to 0.25
- head_bias: float32 [1282], replicated, may hold values from 0.5 to 2.5
Outputs:
- features: bfloat16 [4096, 1024], P(('groups', 'seq', 'head', 'sub')), parts along dimension 0
- waveform: float32 [1310720], P(('groups', 'seq', 'head', 'sub')), parts along dimension 0
There are 2 independent parts, one for each index of `groups`. A program takes and returns all parts, laid end to end along the dimension named above; an argument that names none is the same for every part. Nothing has to cross between parts.
All inputs are finite; a program needn't handle non-finite values. No bound on the sum of `masked` on one device may be relied on, other than what follows from the above.
Results may differ from a plain program's by a relative error of at most 0.02.
Values may be sent and summed in bfloat16 or wider, within the bound.
A program may use at most 64 MiB of HBM per device.

v0:
```python
import math
import jax
import jax.numpy as jnp
from jax import lax
from jax.sharding import PartitionSpec as P

HOP = 320


def with_halo(x, sides, width):
    for axis, dim in sides:
        size, length = (lax.axis_size(axis), x.shape[dim])
        up = [(i, (i + 1) % size) for i in range(size - 1)]
        down = [(j, i) for i, j in up]
        last = lax.slice_in_dim(x, length - width, length, axis=dim)
        initial = lax.slice_in_dim(x, 0, width, axis=dim)
        before = lax.ppermute(last, axis, up)
        after = lax.ppermute(initial, axis, down)
        x = jnp.concatenate([before, x, after], axis=dim)
    return x


def layer_norm(values):
    average = jnp.mean(values, axis=-1, keepdims=True)
    centered = values - average
    return centered * lax.rsqrt(jnp.mean(centered * centered, axis=-1, keepdims=True) + 1e-05)


def unit_heads(projected, head_count):
    row_count = projected.shape[0]
    split_heads = projected.reshape(row_count, head_count, projected.shape[1] // head_count)
    scaled = split_heads * lax.rsqrt(
        jnp.sum(split_heads * split_heads, axis=-1, keepdims=True) + 1e-06
    )
    return scaled.astype(jnp.bfloat16)


def depthwise(kernel, padded_rows):
    tap_count = kernel.shape[0]
    out_rows = padded_rows.shape[0] - tap_count + 1
    result = jnp.zeros((out_rows, padded_rows.shape[1]), jnp.float32)
    for offset in range(tap_count):
        result = result + kernel[offset] * padded_rows[offset : offset + out_rows].astype(
            jnp.float32
        )
    return result


def attend_block(
    paired_sums,
    key_tile_rows,
    value_tile_rows,
    leading_row,
    query_normalized,
    similarity_sharpness,
    frame_ceiling,
):
    weighted, normalizer = paired_sums
    row_count = key_tile_rows.shape[0]
    angular_similarity = jnp.einsum(
        "qhd,khd->hqk", query_normalized, key_tile_rows, preferred_element_type=jnp.float32
    )
    token_position = leading_row + lax.broadcasted_iota(jnp.int32, (1, 1, row_count), 2)
    attention_probabilities = jnp.where(
        token_position < frame_ceiling,
        jnp.exp(similarity_sharpness[:, None, None] * (angular_similarity - 1.0)),
        0.0,
    )
    normalizer = normalizer + jnp.sum(attention_probabilities, axis=2).T
    weighted = weighted + jnp.einsum(
        "hqk,khd->qhd",
        attention_probabilities.astype(jnp.bfloat16),
        value_tile_rows,
        preferred_element_type=jnp.float32,
    )
    return (weighted, normalizer)


def synthesis_tables(bin_count, fft_size):
    bin_ids = lax.broadcasted_iota(jnp.int32, (bin_count, fft_size), 0)
    sample_ids = lax.broadcasted_iota(jnp.int32, (bin_count, fft_size), 1)
    phase_angle = 2.0 * math.pi / fft_size * (bin_ids * sample_ids % fft_size).astype(jnp.float32)
    edge_bin = (bin_ids == 0) | (bin_ids == bin_count - 1)
    factor = jnp.where(edge_bin, 1.0, 2.0) / fft_size
    cos_table = factor * jnp.cos(phase_angle)
    sin_table = jnp.where(edge_bin, 0.0, -factor * jnp.sin(phase_angle))
    return jnp.concatenate([cos_table, sin_table], axis=0)


def local(
    tokens,
    masked,
    used_frames,
    tables,
    mask_vec,
    attn_in,
    head_temp,
    attn_out,
    conv_in,
    conv_kernel,
    conv_out,
    voc_in,
    voc_kernel,
    voc_up,
    voc_down,
    voc_head,
    head_bias,
):
    frame_count = tokens.shape[1]
    group_count = lax.axis_size(("head", "sub"))
    group_index = lax.axis_index(("head", "sub"))
    seq_index = lax.axis_index("seq")
    slab_rows = frame_count // group_count
    frame_ceiling = used_frames[0]
    total_frames = frame_count * lax.axis_size("seq")
    code_ids = lax.broadcasted_iota(jnp.int32, (frame_count, tables.shape[1]), 1)
    masked_rows = masked == 1
    embedded = masked_rows.astype(jnp.float32)[:, None] * mask_vec.astype(jnp.float32)[None, :]
    for rvq_level in range(3):
        matches = tokens[rvq_level][:, None] == code_ids
        if rvq_level == 2:
            matches = matches & jnp.logical_not(masked_rows)[:, None]
        embedded = embedded + jnp.dot(
            matches.astype(jnp.bfloat16), tables[rvq_level], preferred_element_type=jnp.float32
        )
    embedded = embedded.astype(jnp.bfloat16)
    inputs, voc_in_full, voc_up_full, voc_down_full, voc_head_full = (
        lax.all_gather(embedded, ("head", "sub"), axis=1, tiled=True),
        lax.all_gather(voc_in, ("head", "sub"), axis=0, tiled=True),
        lax.all_gather(voc_up, ("head", "sub"), axis=0, tiled=True),
        lax.all_gather(voc_down, ("head", "sub"), axis=0, tiled=True),
        lax.all_gather(voc_head, ("head", "sub"), axis=0, tiled=True),
    )
    normed = layer_norm(inputs.astype(jnp.float32)).astype(jnp.bfloat16)
    local_heads = head_temp.shape[0]
    query_normalized = unit_heads(
        jnp.dot(normed, attn_in[0], preferred_element_type=jnp.float32), local_heads
    )
    key_unit = unit_heads(
        jnp.dot(normed, attn_in[1], preferred_element_type=jnp.float32), local_heads
    ).reshape(frame_count, -1)
    value_rows = jnp.dot(normed, attn_in[2], preferred_element_type=jnp.float32).astype(
        jnp.bfloat16
    )
    head_size = value_rows.shape[1] // local_heads
    start_pair = (
        jnp.zeros((frame_count, local_heads, head_size), jnp.float32),
        jnp.zeros((frame_count, local_heads), jnp.float32),
    )
    paired_sums = start_pair
    key_piece = lax.all_gather(key_unit, "seq", axis=0, tiled=True)
    value_piece = lax.all_gather(value_rows, "seq", axis=0, tiled=True)
    row_count = key_piece.shape[0]
    key_heads = key_piece.reshape(row_count, local_heads, head_size)
    value_heads = value_piece.reshape(row_count, local_heads, head_size)
    block_count = row_count // 512

    def scan_step(inner_pair, block_item):
        key_tile_rows, value_tile_rows, block_index = block_item
        return (
            attend_block(
                inner_pair,
                key_tile_rows,
                value_tile_rows,
                block_index * 512,
                query_normalized,
                head_temp,
                frame_ceiling,
            ),
            None,
        )

    block_items = (
        key_heads.reshape(block_count, 512, local_heads, head_size),
        value_heads.reshape(block_count, 512, local_heads, head_size),
        jnp.arange(block_count, dtype=jnp.int32),
    )
    paired_sums, _unused = lax.scan(scan_step, paired_sums, block_items)
    weighted, normalizer = paired_sums
    attended = (weighted / normalizer[:, :, None]).reshape(frame_count, -1).astype(jnp.bfloat16)
    head_part = jnp.dot(attended, attn_out, preferred_element_type=jnp.float32)
    fft_size = 2 * (head_bias.shape[0] // 2 - 1)
    intersection = fft_size // HOP
    half_voc = voc_kernel.shape[0] // 2
    vocoder_rim = half_voc + intersection // 2
    conv_reach = conv_kernel.shape[0] // 2 + vocoder_rim
    window_rows = slab_rows + 2 * vocoder_rim
    stream = inputs.astype(jnp.float32) + lax.psum(
        head_part.astype(jnp.bfloat16), ("head", "sub")
    ).astype(jnp.float32)
    stream_rims = with_halo(stream.astype(jnp.bfloat16), (("seq", 0),), conv_reach).astype(
        stream.dtype
    )
    conv_normed = layer_norm(stream_rims).astype(jnp.bfloat16)
    residual_window = lax.dynamic_slice_in_dim(
        stream_rims, group_index * slab_rows + conv_reach - vocoder_rim, window_rows, 0
    )
    gate_value = jnp.dot(conv_normed, conv_in[0], preferred_element_type=jnp.float32)
    gate_signal = jnp.dot(conv_normed, conv_in[1], preferred_element_type=jnp.float32)
    gated_rows = (gate_value * jax.nn.sigmoid(gate_signal)).astype(jnp.bfloat16)
    depth_rows = depthwise(conv_kernel, gated_rows)
    activated = (depth_rows * jax.nn.sigmoid(depth_rows)).astype(jnp.bfloat16)
    windows = jnp.stack(
        [
            activated[member * slab_rows : member * slab_rows + window_rows]
            for member in range(group_count)
        ]
    )
    partial_out = jnp.einsum("gsc,cd->gsd", windows, conv_out, preferred_element_type=jnp.float32)
    conv_sum = lax.psum_scatter(
        partial_out.astype(jnp.bfloat16), ("head", "sub"), scatter_dimension=0, tiled=True
    ).astype(jnp.float32)[0]
    block_norm = layer_norm(residual_window + conv_sum).astype(jnp.bfloat16)
    feature_out = block_norm[vocoder_rim : vocoder_rim + slab_rows]
    first_frame = seq_index * frame_count + group_index * slab_rows - vocoder_rim
    frame_ids = first_frame + lax.broadcasted_iota(jnp.int32, (window_rows, 1), 0)
    live_rows = (frame_ids >= 0) & (frame_ids < frame_ceiling)
    base_rows = layer_norm(
        jnp.where(
            live_rows, jnp.dot(block_norm, voc_in_full, preferred_element_type=jnp.float32), 0.0
        )
    )
    vdepth = depthwise(voc_kernel, base_rows)
    voc_rows = vdepth.shape[0]
    inner_rows = layer_norm(vdepth).astype(jnp.bfloat16)
    hidden = jax.nn.gelu(
        jnp.dot(inner_rows, voc_up_full, preferred_element_type=jnp.float32), approximate=False
    ).astype(jnp.bfloat16)
    refined = base_rows[half_voc : half_voc + voc_rows] + jnp.dot(
        hidden, voc_down_full, preferred_element_type=jnp.float32
    )
    head_input = layer_norm(refined).astype(jnp.bfloat16)
    spectrum = jnp.dot(head_input, voc_head_full, preferred_element_type=jnp.float32) + head_bias
    bin_count = spectrum.shape[1] // 2
    magnitude = jnp.minimum(jnp.exp(spectrum[:, :bin_count]), 100.0)
    phase_rows = spectrum[:, bin_count:]
    coefficients = jnp.concatenate(
        [magnitude * jnp.cos(phase_rows), magnitude * jnp.sin(phase_rows)], axis=1
    )
    wave_rows = jnp.dot(
        coefficients, synthesis_tables(bin_count, fft_size), precision=lax.Precision.HIGHEST
    )
    sample_ids = lax.broadcasted_iota(jnp.int32, (fft_size,), 0).astype(jnp.float32)
    hann_window = 0.5 - 0.5 * jnp.cos(2.0 * math.pi / fft_size * sample_ids)
    wave_ids = first_frame + half_voc + lax.broadcasted_iota(jnp.int32, (voc_rows, 1), 0)
    exists = ((wave_ids >= 0) & (wave_ids < total_frames)).astype(jnp.float32)
    framed = (wave_rows * hann_window[None, :] * exists).reshape(voc_rows, intersection, HOP)
    env_rows = (exists * (hann_window * hann_window)[None, :]).reshape(voc_rows, intersection, HOP)
    audio_sum = jnp.zeros((slab_rows, HOP), jnp.float32)
    energy = jnp.zeros((slab_rows, HOP), jnp.float32)
    for quarter in range(intersection):
        begin = intersection - quarter
        audio_sum = audio_sum + framed[begin : begin + slab_rows, quarter]
        energy = energy + env_rows[begin : begin + slab_rows, quarter]
    waveform = (audio_sum / energy).reshape(slab_rows * HOP)
    return (feature_out, waveform)


def solution(mesh):
    in_specs = (
        P(None, ("groups", "seq")),
        P(("groups", "seq")),
        P("groups"),
        P(None, None, ("head", "sub")),
        P(("head", "sub")),
        P(None, None, ("head", "sub")),
        P(("head", "sub")),
        P(("head", "sub"), None),
        P(None, None, ("head", "sub")),
        P(None, ("head", "sub")),
        P(("head", "sub"), None),
        P(("head", "sub"), None),
        P(),
        P(("head", "sub"), None),
        P(("head", "sub"), None),
        P(("head", "sub"), None),
        P(),
    )
    out_specs = (P(("groups", "seq", "head", "sub"), None), P(("groups", "seq", "head", "sub")))
    return jax.shard_map(local, mesh=mesh, in_specs=in_specs, out_specs=out_specs, check_vma=False)
```

profile of v0, /device:TPU:0, one launch (start us, length us, event | category | flops | bytes accessed | tf_op | source)
XLA Modules:
  0.0 276.2 jit_solution(7080855097597714248)
XLA Ops:
  9.4 1.6 fusion.39
  11.0 1.6 fusion.38
  12.6 2.3 fusion.41
  16.1 18.6 %all-gather.6.cloned.1.call-done = bf16[512,1024]{1,0:T(8,128)(2,1)} async-done(((bf16[512,256]{1,0:T(8,128)(2,1)}), bf16[512,1024]{1,0:T(8,128)(2,1)}) %all-gather.6.cloned.1.call-update) | async-done | bytes 1048592 | tf_op jit(solution)/shard_map/all_gather | solution.py:128
  36.2 1.6 fusion.24
  40.1 16.0 %all_gather.23 = bf16[2048,128]{0,1:T(8,128)(2,1)S(1)} all-gather(bf16[512,128]{0,1:T(8,128)(2,1)S(1)} %bitcast.157), channel_id=1, replica_groups=mesh['groups'=2,'seq'=4,'head'=2,'sub'=2] {'seq'}, dimensions={0}, use_global_device_ids=true | all-gather | bytes 655360 | tf_op jit(solution)/shard_map/all_gather | solution.py:151
  57.3 1.9 copy.28
  59.2 2.1 multiply_reduce_fusion.5
  61.4 16.1 %all_gather.22 = bf16[2048,128]{1,0:T(8,128)(2,1)S(1)} all-gather(bf16[512,128]{1,0:T(8,128)(2,1)S(1)} %convolution_convert_fusion.2), channel_id=1, replica_groups=mesh['groups'=2,'seq'=4,'head'=2,'sub'=2] {'seq'}, dimensions={0}, use_global_device_ids=true | all-gather | bytes 655360 | tf_op jit(solution)/shard_map/all_gather | solution.py:152
  79.6 15.6 %while.15 = (s32[]{:T(128)}, f32[512,2,64]{0,2,1:T(8,128)S(1)}, f32[512,2]{0,1:T(2,128)S(1)}, bf16[4,512,2,64]{1,3,2,0:T(8,128)(2,1)S(1)}, s32[4]{0:T(128)S(1)},...) while((s32[]{:T(128)}, f32[512,2,64]{0,2,1:T(8,128)S(1)}, ...), condition=%wide.region_6.7_spmd.clone, body=%wide.region_4.6_spmd.clone.sunk | while | flops 136972288 | bytes 3032748 | solution.py:178
  81.5 1.6 bitcast_reduce_fusion.2
  85.5 1.6 bitcast_reduce_fusion.2
  89.4 1.6 bitcast_reduce_fusion.2
  93.3 1.6 bitcast_reduce_fusion.2
  95.3 2.4 convolution_convert_fusion.1
  97.9 36.0 %all-reduce.2.cloned.1.call-done = bf16[512,1024]{1,0:T(8,128)(2,1)} async-done(((bf16[512,1024]{1,0:T(8,128)(2,1)}), bf16[512,1024]{1,0:T(8,128)(2,1)}) %all-reduce.2.cloned.1.call-update) | async-done | bytes 1048592 | tf_op jit(solution)/shard_map/psum | solution.py:188
  133.9 1.7 fusion.26
  135.6 3.4 %collective-permute-start = (bf16[20,1024]{1,0:T(8,128)(2,1)S(1)}, bf16[20,1024]{1,0:T(8,128)(2,1)S(1)}, u32[]{:S(2)}, u32[]{:S(2)}) collective-permute-start(bf16[20,1024]{1,0:T(8,128)(2,1)S(1)} %get-tuple-element.190), channel_id=1, source_target_pairs={{0,4},{4,8},{8,12},{1,5},{5,9},{9,13},{2,6},{6,10},{10,14},{3,7},{... | collective-permute-start | bytes 122888 | tf_op jit(solution)/shard_map/ppermute | solution.py:17
  140.8 4.3 %collective-permute-done.1 = bf16[20,1024]{1,0:T(8,128)(2,1)S(1)} collective-permute-done((bf16[20,1024]{1,0:T(8,128)(2,1)S(1)}, bf16[20,1024]{1,0:T(8,128)(2,1)S(1)}, u32[]{:S(2)}, u32[]{:S(2)}) %collective-permute-start.1) | collective-permute-done | bytes 40992 | tf_op jit(solution)/shard_map/ppermute | solution.py:18
  147.6 2.3 multiply_convert_fusion.2
  155.0 15.1 %multiply_select_fusion = (f32[641,1280]{1,0:T(8,128)}, f32[641,1280]{1,0:T(8,128)}) fusion(f32[641]{0:T(1024)S(1)} %fusion.133, pred[641]{0:T(1024)(128)(4,1)S(1)} %fusion.132, f32[641]{0:T(1024)S(1)} %select_multiply_fusion), kind=kLoop, calls=%fused_computation.20 | loop fusion | flops 9845760 | bytes 6569609 | tf_op jit(solution)/shard_map/jit(_where)/select_n | solution.py:86
  170.1 1.8 fusion.166
  171.9 4.9 %reduce-scatter.2.cloned.1.call-done = bf16[1,138,1024]{2,1,0:T(8,128)(2,1)} async-done(((bf16[4,138,1024]{2,1,0:T(8,128)(2,1)}), bf16[1,138,1024]{2,1,0:T(8,128)(2,1)}) %reduce-scatter.2.cloned.1.call-update) | async-done | bytes 282640 | tf_op jit(solution)/shard_map/reduce_scatter | solution.py:210
  180.9 14.1 %all-gather.8.cloned.1.call-done = bf16[1024,512]{1,0:T(8,128)(2,1)} async-done(((bf16[256,512]{1,0:T(8,128)(2,1)}), bf16[1024,512]{1,0:T(8,128)(2,1)}) %all-gather.8.cloned.1.call-update) | async-done | bytes 1048592 | tf_op jit(solution)/shard_map/all_gather | solution.py:129
  194.9 1.7 fusion.177
  198.3 17.7 %all-gather.10.cloned.1.call-done = bf16[512,1536]{1,0:T(8,128)(2,1)} async-done(((bf16[128,1536]{1,0:T(8,128)(2,1)}), bf16[512,1536]{1,0:T(8,128)(2,1)}) %all-gather.10.cloned.1.call-update) | async-done | bytes 1572880 | tf_op jit(solution)/shard_map/all_gather | solution.py:130
  216.0 21.1 %all-gather.12.cloned.1.call-done = bf16[1536,512]{1,0:T(8,128)(2,1)} async-done(((bf16[384,512]{1,0:T(8,128)(2,1)}), bf16[1536,512]{1,0:T(8,128)(2,1)}) %all-gather.12.cloned.1.call-update) | async-done | bytes 1572880 | tf_op jit(solution)/shard_map/all_gather | solution.py:131
  237.1 4.3 %fusion.178 = (f32[132]{0:T(256)S(1)}, f32[132,512]{1,0:T(8,128)S(1)}) fusion(bf16[1536,512]{1,0:T(8,128)(2,1)} %all-gather.12.cloned.1.call-done, bf16[512,1536]{1,0:T(8,128)(2,1)} %all-gather.10.cloned.1.call-done, f32[132,512]{1,0:T(8,128)S(1)} %get-tuple-element.185, f32[132]{0:T(256)S(1)} %add_rsqrt_fusion.5, f32[132]{0:T(256)S(1)} %broadcast_multiply_fusion.4, ...), kind=kOutput, calls=%fused_computation.260 | convolution fusion | flops 428752768 | bytes 3958320 | tf_op jit(solution)/shard_map/dot_general | solution.py:229
  241.6 15.4 %all-gather.14.cloned.1.call-done = bf16[512,1282]{0,1:T(8,128)(2,1)} async-done(((bf16[128,1282]{0,1:T(8,128)(2,1)}), bf16[512,1282]{0,1:T(8,128)(2,1)}) %all-gather.14.cloned.1.call-update) | async-done | bytes 1312784 | tf_op jit(solution)/shard_map/all_gather | solution.py:132
  257.0 2.1 convolution_add_fusion
  259.2 1.9 cosine_multiply_fusion.1
  261.1 6.2 %fusion.19 = f32[132,1280]{1,0:T(8,128)S(1)} fusion(f32[641,1280]{1,0:T(8,128)S(1)} %copy-done.2, f32[641,1280]{1,0:T(8,128)} %get-tuple-element.254, f32[132,641]{1,0:T(8,128)S(1)} %get-tuple-element.199, f32[132,641]{1,0:T(8,128)S(1)} %get-tuple-element.198, f32[132]{0:T(256)S(1)} %and_convert_fusion, f32[1280]{0:T(1024)S(1)} %multiply_subtract_fusion), kind=kOutput, calls=%fused_computation.31 | convolution fusion | flops 2601428736 | bytes 7922224 | tf_op jit(solution)/shard_map/dot_general | solution.py:240
  (115 shorter events, 33.3 us)
Async XLA Ops:
  7.2 142.8 %copy-start = (bf16[256,1024]{1,0:T(8,128)(2,1)S(1)}, bf16[256,1024]{1,0:T(8,128)(2,1)}, u32[]{:S(2)}) copy-start(bf16[256,1024]{1,0:T(8,128)(2,1)} %param.29) | copy-start | bytes 1572868
  7.2 27.5 %all-gather.6.cloned.1.call-start = ((), (), s32[]{:S(2)}) async-start(), calls=%async_computation.1 | async-start | bytes 1310720 | tf_op jit(solution)/shard_map/all_gather | solution.py:128
  11.0 4.1 %copy-start.3 = (bf16[3,1024,128]{2,1,0:T(8,128)(2,1)S(1)}, bf16[3,1024,128]{2,1,0:T(8,128)(2,1)}, u32[]{:S(2)}) copy-start(bf16[3,1024,128]{2,1,0:T(8,128)(2,1)} %param.24) | copy-start | bytes 2359300
  14.9 119.0 %all-reduce.2.cloned.1.call-start = ((), (), s32[]{:S(2)}) async-start(), calls=%async_computation.2 | async-start | bytes 2097152 | tf_op jit(solution)/shard_map/psum | solution.py:188
  34.6 3.2 %copy-start.1 = (bf16[512,1024]{1,0:T(8,128)(2,1)S(1)}, bf16[512,1024]{1,0:T(8,128)(2,1)}, u32[]{:S(2)}) copy-start(bf16[512,1024]{1,0:T(8,128)(2,1)} %all-gather.6.cloned.1.call-done) | copy-start | bytes 3145732
  61.4 18.3 %copy-start.8 = (f32[2]{0:T(128)S(1)}, f32[2]{0:T(128)}, u32[]{:S(2)}) copy-start(f32[2]{0:T(128)} %param.25) | copy-start | bytes 28
  95.3 2.6 copy-start.4
  97.8 79.0 %reduce-scatter.2.cloned.1.call-start = ((), (), s32[]{:S(2)}) async-start(), calls=%async_computation.3 | async-start | bytes 1474560 | tf_op jit(solution)/shard_map/reduce_scatter | solution.py:210
  133.9 12.1 %copy-start.7 = (bf16[2,1024,256]{2,1,0:T(8,128)(2,1)S(1)}, bf16[2,1024,256]{2,1,0:T(8,128)(2,1)}, u32[]{:S(2)}) copy-start(bf16[2,1024,256]{2,1,0:T(8,128)(2,1)} %param.27) | copy-start | bytes 3145732
  135.6 5.1 %collective-permute-start = (bf16[20,1024]{1,0:T(8,128)(2,1)S(1)}, bf16[20,1024]{1,0:T(8,128)(2,1)S(1)}, u32[]{:S(2)}, u32[]{:S(2)}) collective-permute-start(bf16[20,1024]{1,0:T(8,128)(2,1)S(1)} %get-tuple-element.190), channel_id=1, source_target_pairs={{0,4},{4,8},{8,12},{1,5},{5,9},{9,13},{2,6},{6,10},{10,14},{3,7},{... | collective-permute-start | bytes 122888 | tf_op jit(solution)/shard_map/ppermute | solution.py:17
  139.0 6.0 %collective-permute-start.1 = (bf16[20,1024]{1,0:T(8,128)(2,1)S(1)}, bf16[20,1024]{1,0:T(8,128)(2,1)S(1)}, u32[]{:S(2)}, u32[]{:S(2)}) collective-permute-start(bf16[20,1024]{1,0:T(8,128)(2,1)S(1)} %get-tuple-element.191), channel_id=1, source_target_pairs={{4,0},{8,4},{12,8},{5,1},{9,5},{13,9},{6,2},{10,6},{14,10},{7,3},{... | collective-permute-start | bytes 122888 | tf_op jit(solution)/shard_map/ppermute | solution.py:18
  149.9 4.8 %copy-start.5 = (f32[7,512]{1,0:T(8,128)S(1)}, f32[7,512]{1,0:T(8,128)}, u32[]{:S(2)}) copy-start(f32[7,512]{1,0:T(8,128)} %param.31) | copy-start | bytes 43012
  151.5 43.5 %all-gather.8.cloned.1.call-start = ((), (), s32[]{:S(2)}) async-start(), calls=%async_computation.4 | async-start | bytes 1310720 | tf_op jit(solution)/shard_map/all_gather | solution.py:129
  152.0 64.0 %all-gather.10.cloned.1.call-start = ((), (), s32[]{:S(2)}) async-start(), calls=%async_computation.5 | async-start | bytes 1966080 | tf_op jit(solution)/shard_map/all_gather | solution.py:130
  152.6 84.5 %all-gather.12.cloned.1.call-start = ((), (), s32[]{:S(2)}) async-start(), calls=%async_computation.6 | async-start | bytes 1966080 | tf_op jit(solution)/shard_map/all_gather | solution.py:131
  153.2 103.8 %all-gather.14.cloned.1.call-start = ((), (), s32[]{:S(2)}) async-start(), calls=%async_computation.7 | async-start | bytes 1648640 | tf_op jit(solution)/shard_map/all_gather | solution.py:132
  198.3 58.8 %copy-start.6 = (f32[1282]{0:T(1024)S(1)}, f32[1282]{0:T(1024)}, u32[]{:S(2)}) copy-start(f32[1282]{0:T(1024)} %param.35) | copy-start | bytes 15388
  257.0 4.0 %copy-start.2 = (f32[641,1280]{1,0:T(8,128)S(1)}, f32[641,1280]{1,0:T(8,128)}, u32[]{:S(2)}) copy-start(f32[641,1280]{1,0:T(8,128)} %get-tuple-element.253) | copy-start | bytes 9845764
Sparse Core Ops, SparseCore 0:
  15.1 19.5 all-gather.5
  97.9 35.9 all-reduce.1
  151.6 25.1 reduce-scatter.1
  178.2 16.6 all-gather.7
  196.3 19.6 all-gather.9
  217.4 19.6 all-gather.11
  238.6 18.3 all-gather.13
where the time goes:
time: 277 us; the launch traced here: 276 us
  waiting for transfers between devices  135 us (49%)
  other arithmetic  38 us (14%)
  matrix products  37 us (13%)
  blocking collectives  32.1 us (12%)
  between operations  15.2 us (5%)
  local copies, waits for them, and re-layouts  11.3 us (4%)
  starting transfers between devices  5.14 us (2%)
  loops' own time  2.77 us (1%)
    psum x1, waiting for transfers between devices, local(): lax.psum(head_part.astype(jnp.bfloat16), ('head', 'sub'))  36 us
    all_gather x1, waiting for transfers between devices, local(): lax.all_gather(voc_down, ('head', 'sub'), axis=0, tiled=True)  21.1 us
    all_gather x1, waiting for transfers between devices, local(): lax.all_gather(embedded, ('head', 'sub'), axis=1, tiled=True)  18.6 us
    all_gather x1, waiting for transfers between devices, local(): lax.all_gather(voc_up, ('head', 'sub'), axis=0, tiled=True)  17.7 us
    all_gather x1, blocking collectives, local(): value_piece = lax.all_gather(value_rows, 'seq', axis=0, tiled=True)  16.1 us
    all_gather x1, blocking collectives, local(): key_piece = lax.all_gather(key_unit, 'seq', axis=0, tiled=True)  16 us
    all_gather x1, waiting for transfers between devices, local(): lax.all_gather(voc_head, ('head', 'sub'), axis=0, tiled=True)  15.4 us
    select_n x1, other arithmetic, synthesis_tables(): sin_table = jnp.where(edge_bin, 0.0, -factor * jnp.sin(phase_angle))  15.1 us
  transfers between devices with their start and end apart: 9, of which 9 were waited for; matrix products, arithmetic and copies ran while one was open for 11% of the time, Pallas kernels for 0%

commit v1 on v0

--- a/solution.py
+++ b/solution.py
@@ -5,6 +5,27 @@
 from jax.sharding import PartitionSpec as P
 
 HOP = 320
+
+
+def collect(shard, axis, dim):
+    size, here, width = (lax.axis_size(axis), lax.axis_index(axis), shard.shape[dim])
+    right = [(i, (i + 1) % size) for i in range(size)]
+    left = [(i, (i - 1) % size) for i in range(size)]
+    whole = jnp.zeros((*shard.shape[:dim], size * width, *shard.shape[dim + 1 :]), shard.dtype)
+    whole = lax.dynamic_update_slice_in_dim(whole, shard, here * width, axis=dim)
+    from_left = from_right = shard
+    half = size // 2
+    for step in range(1, half + 1):
+        from_left = lax.ppermute(from_left, axis, right)
+        whole = lax.dynamic_update_slice_in_dim(
+            whole, from_left, (here - step) % size * width, axis=dim
+        )
+        if step < size - half:
+            from_right = lax.ppermute(from_right, axis, left)
+            whole = lax.dynamic_update_slice_in_dim(
+                whole, from_right, (here + step) % size * width, axis=dim
+            )
+    return whole
 
 
 def with_halo(x, sides, width):
@@ -128,7 +149,7 @@
         lax.all_gather(embedded, ("head", "sub"), axis=1, tiled=True),
         lax.all_gather(voc_in, ("head", "sub"), axis=0, tiled=True),
         lax.all_gather(voc_up, ("head", "sub"), axis=0, tiled=True),
-        lax.all_gather(voc_down, ("head", "sub"), axis=0, tiled=True),
+        collect(voc_down, ("head", "sub"), 0),
         lax.all_gather(voc_head, ("head", "sub"), axis=0, tiled=True),
     )
     normed = layer_norm(inputs.astype(jnp.float32)).astype(jnp.bfloat16)

time: 277 us -> 257 us (0.928)
  waiting for transfers between devices: 135 us -> 107 us
  local copies, waits for them, and re-layouts: 11.3 us -> 17.7 us
    all_gather x1 -> x0, waiting for transfers between devices: 21.1 us -> none  [local(): lax.all_gather(voc_down, ('head', 'sub'), axis=0, tiled=True)]
    dynamic_update_slice x0 -> x4, local copies, waits for them, and re-layouts: none -> 5.1 us  [the longest x2 2.52 us: collect(): lax.dynamic_update_slice_in_dim(whole, from_left, (here - step) % size *...]
    reduce_scatter x1, waiting for transfers between devices: 4.9 us -> 0.01 us  [local(): lax.psum_scatter(partial_out.astype(jnp.bfloat16), ('head', 'sub'), scatt...]
    all_gather x1, waiting for transfers between devices: 14.1 us -> 9.25 us  [local(): lax.all_gather(voc_in, ('head', 'sub'), axis=0, tiled=True)]
    ppermute x0 -> x3, waiting for transfers between devices: none -> 4.6 us  [the longest x2 4.59 us: collect(): from_left = lax.ppermute(from_left, axis, right)]
  transfers between devices with their start and end apart: 9 -> 11, of which waited for: 9 -> 8; matrix products, arithmetic and copies ran while one was open for 11% -> 14% of each run, Pallas kernels for 0% -> 0%
where the time goes in v1:
time: 257 us; the launch traced here: 256 us
  waiting for transfers between devices  107 us (42%)
  other arithmetic  38.5 us (15%)
  matrix products  35.8 us (14%)
  blocking collectives  32.3 us (13%)
  local copies, waits for them, and re-layouts  17.7 us (7%)
  between operations  15.3 us (6%)
  starting transfers between devices  6.77 us (3%)
  loops' own time  2.76 us (1%)
    psum x1, waiting for transfers between devices, local(): lax.psum(head_part.astype(jnp.bfloat16), ('head', 'sub'))  36 us
    all_gather x1, waiting for transfers between devices, local(): lax.all_gather(embedded, ('head', 'sub'), axis=1, tiled=True)  18.6 us
    all_gather x1, waiting for transfers between devices, local(): lax.all_gather(voc_up, ('head', 'sub'), axis=0, tiled=True)  17.7 us
    all_gather x1, blocking collectives, local(): value_piece = lax.all_gather(value_rows, 'seq', axis=0, tiled=True)  16.3 us
    all_gather x1, blocking collectives, local(): key_piece = lax.all_gather(key_unit, 'seq', axis=0, tiled=True)  16 us
    all_gather x1, waiting for transfers between devices, local(): lax.all_gather(voc_head, ('head', 'sub'), axis=0, tiled=True)  15.3 us
    select_n x1, other arithmetic, synthesis_tables(): sin_table = jnp.where(edge_bin, 0.0, -factor * jnp.sin(phase_angle))  15.1 us
    all_gather x1, waiting for transfers between devices, local(): lax.all_gather(voc_in, ('head', 'sub'), axis=0, tiled=True)  9.25 us
  transfers between devices with their start and end apart: 11, of which 8 were waited for; matrix products, arithmetic and copies ran while one was open for 14% of the time, Pallas kernels for 0%

profile of v1, /device:TPU:0, one launch (start us, length us, event | category | flops | bytes accessed | tf_op | source)
XLA Modules:
  0.0 256.3 jit_solution(11266642847124642442)
XLA Ops:
  14.0 18.6 %all-gather.5.cloned.1.call-done = bf16[512,1024]{1,0:T(8,128)(2,1)} async-done(((bf16[512,256]{1,0:T(8,128)(2,1)}), bf16[512,1024]{1,0:T(8,128)(2,1)}) %all-gather.5.cloned.1.call-update) | async-done | bytes 1048592 | tf_op jit(solution)/shard_map/all_gather | solution.py:149
  34.1 1.6 fusion.24
  36.1 2.0 convolution_convert_fusion.2
  38.7 16.0 %all_gather.20 = bf16[2048,128]{0,1:T(8,128)(2,1)S(1)} all-gather(bf16[512,128]{0,1:T(8,128)(2,1)S(1)} %bitcast.157), channel_id=1, replica_groups=mesh['groups'=2,'seq'=4,'head'=2,'sub'=2] {'seq'}, dimensions={0}, use_global_device_ids=true | all-gather | bytes 655360 | tf_op jit(solution)/shard_map/all_gather | solution.py:172
  55.9 1.9 copy.28
  57.8 2.1 multiply_reduce_fusion.5
  59.9 16.3 %all_gather.19 = bf16[2048,128]{1,0:T(8,128)(2,1)S(1)} all-gather(bf16[512,128]{1,0:T(8,128)(2,1)} %convolution_convert_fusion.2), channel_id=1, replica_groups=mesh['groups'=2,'seq'=4,'head'=2,'sub'=2] {'seq'}, dimensions={0}, use_global_device_ids=true | all-gather | bytes 655360 | tf_op jit(solution)/shard_map/all_gather | solution.py:173
  79.0 15.8 %while.15 = (s32[]{:T(128)}, f32[512,2,64]{0,2,1:T(8,128)S(1)}, f32[512,2]{0,1:T(2,128)S(1)}, bf16[4,512,2,64]{1,3,2,0:T(8,128)(2,1)S(1)}, s32[4]{0:T(128)S(1)},...) while((s32[]{:T(128)}, f32[512,2,64]{0,2,1:T(8,128)S(1)}, ...), condition=%wide.region_6.7_spmd.clone, body=%wide.region_4.6_spmd.clone.sunk | while | flops 136972288 | bytes 3032748 | solution.py:199
  80.9 1.7 bitcast_reduce_fusion.2
  84.8 1.7 bitcast_reduce_fusion.2
  88.8 1.7 bitcast_reduce_fusion.2
  92.8 1.7 bitcast_reduce_fusion.2
  94.9 2.4 convolution_convert_fusion.1
  97.4 36.0 %all-reduce.2.cloned.1.call-done = bf16[512,1024]{1,0:T(8,128)(2,1)} async-done(((bf16[512,1024]{1,0:T(8,128)(2,1)}), bf16[512,1024]{1,0:T(8,128)(2,1)}) %all-reduce.2.cloned.1.call-update) | async-done | bytes 1048592 | tf_op jit(solution)/shard_map/psum | solution.py:209
  133.5 1.7 fusion.26
  135.2 3.4 %collective-permute-start = (bf16[20,1024]{1,0:T(8,128)(2,1)S(1)}, bf16[20,1024]{1,0:T(8,128)(2,1)S(1)}, u32[]{:S(2)}, u32[]{:S(2)}) collective-permute-start(bf16[20,1024]{1,0:T(8,128)(2,1)S(1)} %get-tuple-element.190), channel_id=1, source_target_pairs={{0,4},{4,8},{8,12},{1,5},{5,9},{9,13},{2,6},{6,10},{10,14},{3,7},{... | collective-permute-start | bytes 122888 | tf_op jit(solution)/shard_map/ppermute | solution.py:38
  140.3 4.3 %collective-permute-done.1 = bf16[20,1024]{1,0:T(8,128)(2,1)S(1)} collective-permute-done((bf16[20,1024]{1,0:T(8,128)(2,1)S(1)}, bf16[20,1024]{1,0:T(8,128)(2,1)S(1)}, u32[]{:S(2)}, u32[]{:S(2)}) %collective-permute-start.1) | collective-permute-done | bytes 40992 | tf_op jit(solution)/shard_map/ppermute | solution.py:39
  147.1 2.3 multiply_convert_fusion.2
  152.3 1.7 collective-permute-start.3
  154.2 15.1 %multiply_select_fusion = (f32[641,1280]{1,0:T(8,128)}, f32[641,1280]{1,0:T(8,128)}) fusion(f32[641]{0:T(1024)S(1)} %fusion.133, pred[641]{0:T(1024)(128)(4,1)S(1)} %fusion.132, f32[641]{0:T(1024)S(1)} %select_multiply_fusion), kind=kLoop, calls=%fused_computation.20 | loop fusion | flops 9845760 | bytes 6569609 | tf_op jit(solution)/shard_map/jit(_where)/select_n | solution.py:107
  173.2 1.8 constant_dynamic-update-slice_fusion.1
  175.0 4.6 %collective-permute-done.4 = bf16[384,512]{1,0:T(8,128)(2,1)} collective-permute-done((bf16[384,512]{1,0:T(8,128)(2,1)S(1)}, bf16[384,512]{1,0:T(8,128)(2,1)}, u32[]{:S(2)}, u32[]{:S(2)}) %collective-permute-start.4) | collective-permute-done | bytes 393248 | tf_op jit(solution)/shard_map/ppermute | solution.py:19
  179.6 1.8 constant_dynamic-update-slice_fusion
  181.3 1.8 fusion.166
  187.2 9.3 %all-gather.7.cloned.1.call-done = bf16[1024,512]{1,0:T(8,128)(2,1)} async-done(((bf16[256,512]{1,0:T(8,128)(2,1)}), bf16[1024,512]{1,0:T(8,128)(2,1)}) %all-gather.7.cloned.1.call-update) | async-done | bytes 1048592 | tf_op jit(solution)/shard_map/all_gather | solution.py:150
  196.5 1.7 fusion.177
  199.8 17.7 %all-gather.9.cloned.1.call-done = bf16[512,1536]{1,0:T(8,128)(2,1)} async-done(((bf16[128,1536]{1,0:T(8,128)(2,1)}), bf16[512,1536]{1,0:T(8,128)(2,1)}) %all-gather.9.cloned.1.call-update) | async-done | bytes 1572880 | tf_op jit(solution)/shard_map/all_gather | solution.py:151
  217.6 4.3 %fusion.178 = (f32[132]{0:T(256)S(1)}, f32[132,512]{1,0:T(8,128)S(1)}) fusion(bf16[1536,512]{1,0:T(8,128)(2,1)} %constant_dynamic-update-slice_fusion, bf16[512,1536]{1,0:T(8,128)(2,1)} %all-gather.9.cloned.1.call-done, f32[132,512]{1,0:T(8,128)S(1)} %get-tuple-element.185, f32[132]{0:T(256)S(1)} %add_rsqrt_fusion.5, f32[132]{0:T(256)S(1)} %broadcast_multiply_fusion.4, ...), kind=kOutput, calls=%fused_computation.264 | convolution fusion | flops 428752768 | bytes 3958320 | tf_op jit(solution)/shard_map/dot_general | solution.py:250
  222.1 15.3 %all-gather.11.cloned.1.call-done = bf16[512,1282]{0,1:T(8,128)(2,1)} async-done(((bf16[128,1282]{0,1:T(8,128)(2,1)}), bf16[512,1282]{0,1:T(8,128)(2,1)}) %all-gather.11.cloned.1.call-update) | async-done | bytes 1312784 | tf_op jit(solution)/shard_map/all_gather | solution.py:153
  237.4 2.1 convolution_add_fusion
  239.5 1.7 cosine_multiply_fusion.1
  241.2 6.2 %fusion.19 = f32[132,1280]{1,0:T(8,128)S(1)} fusion(f32[641,1280]{1,0:T(8,128)S(1)} %copy-done.2, f32[641,1280]{1,0:T(8,128)} %get-tuple-element.254, f32[132,641]{1,0:T(8,128)S(1)} %get-tuple-element.199, f32[132,641]{1,0:T(8,128)S(1)} %get-tuple-element.198, f32[132]{0:T(256)S(1)} %and_convert_fusion, f32[1280]{0:T(1024)S(1)} %multiply_subtract_fusion), kind=kOutput, calls=%fused_computation.31 | convolution fusion | flops 2601428736 | bytes 7922224 | tf_op jit(solution)/shard_map/dot_general | solution.py:261
  (127 shorter events, 37.7 us)
Async XLA Ops:
  7.2 142.3 %copy-start = (bf16[256,1024]{1,0:T(8,128)(2,1)S(1)}, bf16[256,1024]{1,0:T(8,128)(2,1)}, u32[]{:S(2)}) copy-start(bf16[256,1024]{1,0:T(8,128)(2,1)} %param.29) | copy-start | bytes 1572868
  7.2 25.4 %all-gather.5.cloned.1.call-start = ((), (), s32[]{:S(2)}) async-start(), calls=%async_computation.1 | async-start | bytes 1310720 | tf_op jit(solution)/shard_map/all_gather | solution.py:149
  7.2 3.8 %copy-start.8 = (bf16[3,1024,256]{2,1,0:T(8,128)(2,1)S(1)}, bf16[3,1024,256]{2,1,0:T(8,128)(2,1)}, u32[]{:S(2)}) copy-start(bf16[3,1024,256]{2,1,0:T(8,128)(2,1)} %param.22) | copy-start | bytes 4718596
  11.0 1.9 copy-start.4
  12.9 120.6 %all-reduce.2.cloned.1.call-start = ((), (), s32[]{:S(2)}) async-start(), calls=%async_computation.2 | async-start | bytes 2097152 | tf_op jit(solution)/shard_map/psum | solution.py:209
  32.6 3.2 %copy-start.1 = (bf16[512,1024]{1,0:T(8,128)(2,1)S(1)}, bf16[512,1024]{1,0:T(8,128)(2,1)}, u32[]{:S(2)}) copy-start(bf16[512,1024]{1,0:T(8,128)(2,1)} %all-gather.5.cloned.1.call-done) | copy-start | bytes 3145732
  59.9 19.1 %copy-start.10 = (f32[2]{0:T(128)S(1)}, f32[2]{0:T(128)}, u32[]{:S(2)}) copy-start(f32[2]{0:T(128)} %param.25) | copy-start | bytes 28
  94.8 2.6 copy-start.5
  97.3 85.8 %reduce-scatter.2.cloned.1.call-start = ((), (), s32[]{:S(2)}) async-start(), calls=%async_computation.3 | async-start | bytes 1474560 | tf_op jit(solution)/shard_map/reduce_scatter | solution.py:231
  133.5 12.1 %copy-start.9 = (bf16[2,1024,256]{2,1,0:T(8,128)(2,1)S(1)}, bf16[2,1024,256]{2,1,0:T(8,128)(2,1)}, u32[]{:S(2)}) copy-start(bf16[2,1024,256]{2,1,0:T(8,128)(2,1)} %param.27) | copy-start | bytes 3145732
  135.2 5.1 %collective-permute-start = (bf16[20,1024]{1,0:T(8,128)(2,1)S(1)}, bf16[20,1024]{1,0:T(8,128)(2,1)S(1)}, u32[]{:S(2)}, u32[]{:S(2)}) collective-permute-start(bf16[20,1024]{1,0:T(8,128)(2,1)S(1)} %get-tuple-element.190), channel_id=1, source_target_pairs={{0,4},{4,8},{8,12},{1,5},{5,9},{9,13},{2,6},{6,10},{10,14},{3,7},{... | collective-permute-start | bytes 122888 | tf_op jit(solution)/shard_map/ppermute | solution.py:38
  138.6 6.0 %collective-permute-start.1 = (bf16[20,1024]{1,0:T(8,128)(2,1)S(1)}, bf16[20,1024]{1,0:T(8,128)(2,1)S(1)}, u32[]{:S(2)}, u32[]{:S(2)}) collective-permute-start(bf16[20,1024]{1,0:T(8,128)(2,1)S(1)} %get-tuple-element.191), channel_id=1, source_target_pairs={{4,0},{8,4},{12,8},{5,1},{9,5},{13,9},{6,2},{10,6},{14,10},{7,3},{... | collective-permute-start | bytes 122888 | tf_op jit(solution)/shard_map/ppermute | solution.py:39
  149.5 2.8 %copy-start.3 = (bf16[384,512]{1,0:T(8,128)(2,1)S(1)}, bf16[384,512]{1,0:T(8,128)(2,1)}, u32[]{:S(2)}) copy-start(bf16[384,512]{1,0:T(8,128)(2,1)} %param.33) | copy-start | bytes 1179652
  149.5 4.7 %copy-start.6 = (f32[7,512]{1,0:T(8,128)S(1)}, f32[7,512]{1,0:T(8,128)}, u32[]{:S(2)}) copy-start(f32[7,512]{1,0:T(8,128)} %param.31) | copy-start | bytes 43012
  151.0 45.5 %all-gather.7.cloned.1.call-start = ((), (), s32[]{:S(2)}) async-start(), calls=%async_computation.4 | async-start | bytes 1310720 | tf_op jit(solution)/shard_map/all_gather | solution.py:150
  151.6 66.0 %all-gather.9.cloned.1.call-start = ((), (), s32[]{:S(2)}) async-start(), calls=%async_computation.5 | async-start | bytes 1966080 | tf_op jit(solution)/shard_map/all_gather | solution.py:151
  152.2 85.2 %all-gather.11.cloned.1.call-start = ((), (), s32[]{:S(2)}) async-start(), calls=%async_computation.6 | async-start | bytes 1648640 | tf_op jit(solution)/shard_map/all_gather | solution.py:153
  152.3 18.0 %collective-permute-start.2 = (bf16[384,512]{1,0:T(8,128)(2,1)S(1)}, bf16[384,512]{1,0:T(8,128)(2,1)S(1)}, u32[]{:S(2)}, u32[]{:S(2)}) collective-permute-start(bf16[384,512]{1,0:T(8,128)(2,1)S(1)} %copy-done.3), channel_id=1, source_target_pairs={{0,1},{1,2},{2,3},{3,0},{4,5},{5,6},{6,7},{7,4},{8,9},{9,10},{10,1... | collective-permute-start | bytes 1179656 | tf_op jit(solution)/shard_map/ppermute | solution.py:19
  152.3 20.9 %collective-permute-start.3 = (bf16[384,512]{1,0:T(8,128)(2,1)S(1)}, bf16[384,512]{1,0:T(8,128)(2,1)}, u32[]{:S(2)}, u32[]{:S(2)}) collective-permute-start(bf16[384,512]{1,0:T(8,128)(2,1)S(1)} %copy-done.3), channel_id=1, source_target_pairs={{0,3},{1,0},{2,1},{3,2},{4,7},{5,4},{6,5},{7,6},{8,11},{9,8},{10,9... | collective-permute-start | bytes 1179656 | tf_op jit(solution)/shard_map/ppermute | solution.py:24
  170.2 9.3 %collective-permute-start.4 = (bf16[384,512]{1,0:T(8,128)(2,1)S(1)}, bf16[384,512]{1,0:T(8,128)(2,1)}, u32[]{:S(2)}, u32[]{:S(2)}) collective-permute-start(bf16[384,512]{1,0:T(8,128)(2,1)S(1)} %collective-permute-done.2), channel_id=1, source_target_pairs={{0,1},{1,2},{2,3},{3,0},{4,5},{5,6},{6,7},{7,4},{8,9},{9,10},{10,1... | collective-permute-start | bytes 1179656 | tf_op jit(solution)/shard_map/ppermute | solution.py:19
  199.8 37.6 %copy-start.7 = (f32[1282]{0:T(1024)S(1)}, f32[1282]{0:T(1024)}, u32[]{:S(2)}) copy-start(f32[1282]{0:T(1024)} %param.35) | copy-start | bytes 15388
  237.4 3.8 %copy-start.2 = (f32[641,1280]{1,0:T(8,128)S(1)}, f32[641,1280]{1,0:T(8,128)}, u32[]{:S(2)}) copy-start(f32[641,1280]{1,0:T(8,128)} %get-tuple-element.253) | copy-start | bytes 9845764
Sparse Core Ops, SparseCore 0:
  13.0 19.5 all-gather.4
  97.4 35.9 all-reduce.1
  151.2 26.2 reduce-scatter.1
  178.9 17.5 all-gather.6
  197.9 19.6 all-gather.8
  219.0 18.3 all-gather.10
